TPU v7x, 32 devices: a whole 2x2x4 slice. The times are simulated.
32 devices in a mesh: depth: 8 (over z, core), freq: 4 (over y, x).
Axes of the slice: x: 2, y: 2, z: 4, core: 2. Of those that a mesh axis runs over, the one named last changes fastest.
Arguments:
- fields_top: bfloat16 [8, 2, 4, 2, 384, 384], P('depth', None, 'freq'), may hold values from -6 to 6
- surface: bfloat16 [2, 2, 4, 2, 384, 384], P(None, None, 'freq'), may hold values from -6 to 6
- up_state: bfloat16 [8, 4, 2, 384, 384], P('depth', 'freq'), may hold values from -6 to 6
- angular_freq: float32 [4], P('freq'), may hold values from 0.5 to 2.5
- class_slowness: float32 [8], replicated, may hold values from 0.6 to 1.3
- velocity_class: int32 [8, 12, 12], P('depth'), may hold values from 0 to 7
- slowness_detail: float32 [8, 384, 384], P('depth'), may hold values from 0.5 to 1.5
Outputs:
- reflectivity: bfloat16 [8, 384, 384], P('depth', 'freq')
- up_out: bfloat16 [8, 4, 2, 384, 384], P('depth', 'freq')
All inputs are finite; a program needn't handle non-finite values.
Results may differ from a plain program's by a relative error of at most 0.023.
Values may be sent and summed in bfloat16 or wider, within the bound.
A program may use at most 64 MiB of HBM per device.

v0:
```python
import jax
import jax.numpy as jnp
from jax import lax
from jax.sharding import PartitionSpec as P

LAYERS = 1
TICKS = 3
CLASSES = 8
BLOCK = 32
DEPTH_STEP = 1.0
EPSILON = 1e-06


def passed_along(block, axis, distance):
    devices = range(lax.axis_size(axis))
    route = [(i - distance, i) for i in devices if i - distance in devices]
    return lax.ppermute(block, axis, route)


def make_tables(lateral):
    positions = jnp.arange(lateral, dtype=jnp.int32)
    wrapped = positions[:, None] * positions[None, :] % lateral
    angles = wrapped.astype(jnp.float32) * (2.0 * jnp.pi / lateral)
    cosine_table = jnp.cos(angles).astype(jnp.bfloat16)
    sine_table = jnp.sin(angles).astype(jnp.bfloat16)
    folded = jnp.where(positions < lateral // 2, positions, positions - lateral)
    kappa = folded.astype(jnp.float32) * (2.0 * jnp.pi / lateral)
    wavenumber_sq = kappa[:, None] ** 2 + kappa[None, :] ** 2
    return (cosine_table, sine_table, wavenumber_sq)


def cell_slowness(velocity_class, class_slowness, slowness_detail):
    count, lateral = (slowness_detail.shape[0], slowness_detail.shape[1])
    blocks = lateral // BLOCK
    onehot = (velocity_class[..., None] == jnp.arange(CLASSES, dtype=jnp.int32)).astype(jnp.float32)
    block_slow = jnp.sum(onehot * class_slowness, axis=-1)
    spread = jnp.broadcast_to(
        block_slow[:, :, None, :, None], (count, blocks, BLOCK, blocks, BLOCK)
    )
    slowness = spread.reshape(count, lateral, lateral) * slowness_detail
    return (slowness, jnp.mean(slowness, axis=(1, 2)))


def propagate(
    real_part, imag_part, angular, slowness, reference_slow, cosine_table, sine_table, wavenumber_sq
):
    lateral = real_part.shape[0]
    joined_cols = jnp.concatenate([cosine_table, sine_table], axis=1)
    joined_rows = jnp.concatenate([cosine_table, sine_table], axis=0)
    product = jnp.dot(
        jnp.concatenate([real_part, imag_part], axis=0),
        joined_cols,
        preferred_element_type=jnp.float32,
    )
    real_cos, real_sin = (product[:lateral, :lateral], product[:lateral, lateral:])
    imag_cos, imag_sin = (product[lateral:, :lateral], product[lateral:, lateral:])
    half_real = (real_cos + imag_sin).astype(jnp.bfloat16)
    half_imag = (imag_cos - real_sin).astype(jnp.bfloat16)
    product = jnp.dot(
        joined_rows,
        jnp.concatenate([half_real, half_imag], axis=1),
        preferred_element_type=jnp.float32,
    )
    cos_real, cos_imag = (product[:lateral, :lateral], product[:lateral, lateral:])
    sin_real, sin_imag = (product[lateral:, :lateral], product[lateral:, lateral:])
    spec_real = cos_real + sin_imag
    spec_imag = cos_imag - sin_real
    vertical = (angular * reference_slow) ** 2 - wavenumber_sq
    travel = jnp.sqrt(jnp.maximum(vertical, 0.0)) * DEPTH_STEP
    decay = jnp.exp(-jnp.sqrt(jnp.maximum(-vertical, 0.0)) * DEPTH_STEP) / (lateral * lateral)
    phase_real = decay * jnp.cos(travel)
    phase_imag = decay * jnp.sin(travel)
    shifted_real = (spec_real * phase_real - spec_imag * phase_imag).astype(jnp.bfloat16)
    shifted_imag = (spec_real * phase_imag + spec_imag * phase_real).astype(jnp.bfloat16)
    product = jnp.dot(
        joined_rows,
        jnp.concatenate([shifted_real, shifted_imag], axis=1),
        preferred_element_type=jnp.float32,
    )
    cos_real, cos_imag = (product[:lateral, :lateral], product[:lateral, lateral:])
    sin_real, sin_imag = (product[lateral:, :lateral], product[lateral:, lateral:])
    back_real = (cos_real - sin_imag).astype(jnp.bfloat16)
    back_imag = (cos_imag + sin_real).astype(jnp.bfloat16)
    product = jnp.dot(
        jnp.concatenate([back_real, back_imag], axis=0),
        joined_cols,
        preferred_element_type=jnp.float32,
    )
    real_cos, real_sin = (product[:lateral, :lateral], product[:lateral, lateral:])
    imag_cos, imag_sin = (product[lateral:, :lateral], product[lateral:, lateral:])
    space_real = real_cos - imag_sin
    space_imag = imag_cos + real_sin
    lens = angular * DEPTH_STEP * (slowness - reference_slow)
    lens_cos, lens_sin = (jnp.cos(lens), jnp.sin(lens))
    new_real = (space_real * lens_cos - space_imag * lens_sin).astype(jnp.bfloat16)
    new_imag = (space_real * lens_sin + space_imag * lens_cos).astype(jnp.bfloat16)
    return (new_real, new_imag)


def advance(fields, angular, slowness, reference_slow, tables):
    cosine_table, sine_table, wavenumber_sq = tables

    def single(real_part, imag_part, frequency):
        return propagate(
            real_part,
            imag_part,
            frequency,
            slowness,
            reference_slow,
            cosine_table,
            sine_table,
            wavenumber_sq,
        )

    new_real, new_imag = jax.vmap(single)(fields[:, 0], fields[:, 1], angular)
    return jnp.stack([new_real, new_imag], axis=1)


def advance_pair(fields, angular, slowness, reference_slow, tables):

    def one_field(member):
        return advance(member, angular, slowness, reference_slow, tables)

    return jax.vmap(one_field)(fields)


def image_terms(fields):
    source = fields[0].astype(jnp.float32)
    receiver = fields[1].astype(jnp.float32)
    image_part = jnp.sum(source[:, 0] * receiver[:, 0] + source[:, 1] * receiver[:, 1], axis=0)
    illum_part = jnp.sum(source[:, 0] * source[:, 0] + source[:, 1] * source[:, 1], axis=0)
    return (image_part, illum_part)


def per_device(
    fields_top, surface, up_state, angular_freq, class_slowness, velocity_class, slowness_detail
):
    lateral = fields_top.shape[-1]
    tables = make_tables(lateral)
    slowness, reference_slow = cell_slowness(velocity_class, class_slowness, slowness_detail)
    segment_index = lax.axis_index("depth")
    image_sum = [jnp.zeros((lateral, lateral), jnp.float32)]
    illumination = [jnp.zeros((lateral, lateral), jnp.float32)]
    sources = [None] * LAYERS
    fields = fields_top[0]
    for turn_index in range(TICKS):
        layer_index = 0
        fields = advance_pair(
            fields, angular_freq, slowness[layer_index], reference_slow[layer_index], tables
        )
        image_part, illum_part = image_terms(fields)
        image_sum[layer_index] = image_sum[layer_index] + image_part
        illumination[layer_index] = illumination[layer_index] + illum_part
        if turn_index == TICKS - 1:
            sources[layer_index] = fields[0]
        if turn_index + 1 < TICKS:
            from_above = passed_along(fields, "depth", 1)
            fields = jnp.where(segment_index == 0, surface[turn_index], from_above)
    image_all = jnp.stack(image_sum)
    illum_all = jnp.stack(illumination)
    image_total, illum_total = (
        lax.psum(image_all.astype(jnp.bfloat16), "freq").astype(jnp.float32),
        lax.psum(illum_all.astype(jnp.bfloat16), "freq").astype(jnp.float32),
    )
    damping = jnp.mean(illum_total, axis=(1, 2))
    balanced = image_total / (illum_total + damping[:, None, None])
    mean_square = jnp.mean(balanced * balanced, axis=(1, 2))
    reflect = (balanced * lax.rsqrt(mean_square + EPSILON)[:, None, None]).astype(jnp.bfloat16)
    row_count = lateral // lax.axis_size("freq")
    reflect_part = lax.dynamic_slice_in_dim(
        reflect, lax.axis_index("freq") * row_count, row_count, 1
    )
    rising_wave = passed_along(up_state[0], "depth", -1)
    for layer_index in reversed(range(LAYERS)):
        scattered = reflect[layer_index].astype(jnp.float32)[None, None] * sources[
            layer_index
        ].astype(jnp.float32)
        rising_wave = (rising_wave.astype(jnp.float32) + scattered).astype(jnp.bfloat16)
        rising_wave = advance(
            rising_wave, angular_freq, slowness[layer_index], reference_slow[layer_index], tables
        )
    return (reflect_part, rising_wave[None])


def solution(mesh):
    return jax.shard_map(
        per_device,
        mesh=mesh,
        in_specs=(
            P("depth", None, "freq", None, None, None),
            P(None, None, "freq", None, None, None),
            P("depth", "freq", None, None, None),
            P("freq"),
            P(),
            P("depth", None, None),
            P("depth", None, None),
        ),
        out_specs=(P("depth", "freq", None), P("depth", "freq", None, None, None)),
        check_vma=False,
    )
```

profile of v0, /device:TPU:0, one launch (start us, length us, event | category | flops | bytes accessed | tf_op | source)
XLA Modules:
  0.0 157.0 jit_solution(17389596648066102286)
XLA Ops:
  7.2 2.6 %sine_convert_fusion = (bf16[384,384]{0,1:T(8,128)(2,1)S(1)}, bf16[384,384]{0,1:T(8,128)(2,1)S(1)}) fusion(), kind=kLoop, calls=%fused_computation.237 | loop fusion | flops 1622016 | bytes 589824 | tf_op jit(solution)/shard_map/convert_element_type | solution.py:25
  11.2 1.9 %broadcast_in_dim.6 = f32[12,32,12,32]{3,2,1,0:T(8,128)} broadcast(f32[12,12]{1,0:T(8,128)S(1)} %select_reduce_fusion), dimensions={0,2} | broadcast | bytes 590400 | tf_op jit(solution)/shard_map/broadcast_in_dim | solution.py:37
  13.1 2.5 %broadcast_in_dim.7 = f32[1,384,384]{2,1,0:T(8,128)S(1)} reshape(f32[12,32,12,32]{3,2,1,0:T(8,128)} %broadcast_in_dim.6) | data formatting | bytes 1179648 | tf_op jit(solution)/shard_map/broadcast_in_dim | solution.py:37
  18.1 1.4 convolution_bitcast_fusion.11
  19.8 2.6 %cosine_multiply_fusion.1 = (f32[384,384]{0,1:T(8,128)S(1)}, f32[384,384]{0,1:T(8,128)S(1)}) fusion(f32[384]{0:T(512)S(1)} %fusion.123, f32[]{:T(128)} %bitcast.11), kind=kLoop, calls=%fused_computation.233 | loop fusion | flops 1327104 | bytes 1181188 | tf_op jit(solution)/shard_map/vmap(vmap())/mul | solution.py:71
  22.3 1.4 convolution_bitcast_fusion.10
  24.1 1.4 convolution_bitcast_fusion.9
  25.8 2.3 %fusion.113 = (f32[384,384]{1,0:T(8,128)S(1)}, f32[384,384]{1,0:T(8,128)S(1)}) fusion(f32[1,384,384]{2,1,0:T(8,128)S(1)} %get-tuple-element.7, f32[]{:T(128)} %div.22, f32[]{:T(128)} %bitcast.257), kind=kLoop, calls=%fused_computation.245 | loop fusion | flops 294912 | bytes 1769480 | tf_op jit(solution)/shard_map/vmap(vmap())/mul | solution.py:95
  28.1 1.4 convolution_bitcast_fusion.8
  30.0 1.2 pad_maximum_fusion
  31.2 3.4 %collective-permute-start = (bf16[2,1,2,384,384]{4,3,0,2,1:T(8,128)(2,1)}, bf16[2,1,2,384,384]{4,3,0,2,1:T(8,128)(2,1)}, u32[]{:S(2)}, u32[]{:S(2)}) collective-permute-start(bf16[2,1,2,384,384]{4,3,0,2,1:T(8,128)(2,1)} %pad_maximum_fusion), channel_id=1, source_target_pairs={{0,4},{4,8},{8,12},{12,16},{16,20},{20,24},{24,28},{1,5},{5,9},{9,... | collective-permute-start | bytes 3538952 | tf_op jit(solution)/shard_map/ppermute | solution.py:17
  34.6 1.9 %fusion.141 = (bf16[1,2,1,2,384,384]{5,4,3,2,1,0:T(8,128)(2,1)S(1)}, bf16[1,2,1,2,384,384]{5,4,3,2,1,0:T(8,128)(2,1)S(1)}) fusion(bf16[2,2,1,2,384,384]{5,4,3,2,1,0:T(8,128)(2,1)} %param.8), kind=kLoop, calls=%fused_computation.281 | loop fusion | bytes 4718592 | tf_op jit(solution)/shard_map/slice | solution.py:158
  36.8 1.4 convolution_bitcast_fusion.7
  38.5 1.4 convolution_bitcast_fusion.6
  40.3 1.4 convolution_bitcast_fusion.5
  42.0 1.4 convolution_bitcast_fusion.4
  44.0 16.8 %collective-permute-start.1 = (bf16[2,1,2,384,384]{4,3,0,2,1:T(8,128)(2,1)S(1)}, bf16[2,1,2,384,384]{4,3,0,2,1:T(8,128)(2,1)S(1)}, u32[]{:S(2)}, u32[]{:S(2)}) collective-permute-start(bf16[2,1,2,384,384]{4,3,0,2,1:T(8,128)(2,1)S(1)} %pad_maximum_fusion.1), channel_id=1, source_target_pairs={{0,4},{4,8},{8,12},{12,16},{16,20},{20,24},{24,28},{1,5},{5,9},{9,... | collective-permute-start | bytes 3538952 | tf_op jit(solution)/shard_map/ppermute | solution.py:17
  61.1 1.8 %collective-permute-done.1 = bf16[2,1,2,384,384]{4,3,0,2,1:T(8,128)(2,1)S(1)} collective-permute-done((bf16[2,1,2,384,384]{4,3,0,2,1:T(8,128)(2,1)S(1)}, bf16[2,1,2,384,384]{4,3,0,2,1:T(8,128)(2,1)S(1)}, u32[]{:S(2)}, u32[]{:S(2)}) %collective-permute-start.1) | collective-permute-done | bytes 1179680 | tf_op jit(solution)/shard_map/ppermute | solution.py:17
  63.2 1.4 convolution_bitcast_fusion.3
  64.9 1.4 convolution_bitcast_fusion.2
  66.7 1.4 convolution_bitcast_fusion.1
  68.4 1.4 convolution_bitcast_fusion
  70.4 1.3 fusion.120
  71.7 1.6 collective-permute-start.2
  73.3 59.8 %all-reduce.3.cloned.1.call-done = (bf16[1,384,384]{2,1,0:T(8,128)(2,1)}, bf16[1,384,384]{2,1,0:T(8,128)(2,1)}) async-done(((bf16[1,384,384]{2,1,0:T(8,128)(2,1)}, bf16[1,384,384]{2,1,0:T(8,128)(2,1)}), (bf16[1,384,384]{2,1,0:T(8,128)(2,1)}, bf16[1,384,384]{2,1,0:T(8,128)(2,1)})) %all-reduce.3.cloned.1.call-update) | async-done | bytes 589840 | tf_op jit(solution)/shard_map/psum | solution.py:163
  133.1 1.7 %convert_reduce_fusion = f32[]{:T(128)} fusion(bf16[1,384,384]{2,1,0:T(8,128)(2,1)} %get-tuple-element.2), kind=kLoop, calls=%fused_computation.120 | loop fusion | flops 294911 | bytes 294916 | tf_op jit(solution)/shard_map/reduce_sum | solution.py:165
  135.5 1.8 %multiply_reduce_fusion = f32[]{:T(128)} fusion(f32[]{:T(128)S(6)} %div.25, bf16[1,384,384]{2,1,0:T(8,128)(2,1)} %get-tuple-element.2, bf16[1,384,384]{2,1,0:T(8,128)(2,1)} %get-tuple-element.3), kind=kLoop, calls=%fused_computation.229 | loop fusion | flops 884735 | bytes 589832 | tf_op jit(solution)/shard_map/reduce_sum | solution.py:167
  138.0 1.2 bitcast_convert_fusion
  141.1 3.1 %subtract_convert_fusion.7 = (bf16[1,384,384]{1,2,0:T(8,128)(2,1)S(1)}, bf16[1,384,384]{1,2,0:T(8,128)(2,1)S(1)}) fusion(f32[384]{0:T(512)S(1)} %fusion.123, f32[]{:T(128)} %bitcast.11, f32[768,1,768]{0,2,1:T(8,128)S(1)} %convolution_bitcast_fusion.12), kind=kLoop, calls=%fused_computation.222 | loop fusion | flops 2801664 | bytes 2953220 | tf_op jit(solution)/shard_map/vmap()/convert_element_type | solution.py:73
  144.3 0.8 convolution_bitcast_fusion.14
  146.9 2.3 %fusion.117 = (bf16[1,1,384,384]{3,2,1,0:T(8,128)(2,1)S(1)}, bf16[1,1,384,384]{3,2,1,0:T(8,128)(2,1)S(1)}) fusion(f32[1,384,384]{2,1,0:T(8,128)S(1)} %copy-done.3, f32[]{:T(128)} %div.22, f32[]{:T(128)} %bitcast.258, f32[1,768,768]{2,1,0:T(8,128)S(1)} %convolution_bitcast_fusion.13), kind=kLoop, calls=%fused_computation.252 | loop fusion | flops 1769472 | bytes 3538952 | tf_op jit(solution)/shard_map/stack | solution.py:116
  149.3 0.9 maximum_bitcast_fusion.32
  (52 shorter events, 11.4 us)
Async XLA Ops:
  7.2 125.9 %all-reduce.3.cloned.1.call-start = ((), (), s32[]{:S(2)}) async-start(), calls=%async_computation | async-start | bytes 1179648 | tf_op jit(solution)/shard_map/psum | solution.py:163
  13.1 3.3 %copy-start.5 = (f32[1,384,384]{2,1,0:T(8,128)S(1)}, f32[1,384,384]{2,1,0:T(8,128)}, u32[]{:S(2)}) copy-start(f32[1,384,384]{2,1,0:T(8,128)} %param.13) | copy-start | bytes 1769476
  15.6 2.2 %copy-start.4 = (bf16[1,2,1,2,384,384]{5,4,3,2,1,0:T(8,128)(2,1)S(1)}, bf16[1,2,1,2,384,384]{5,4,3,2,1,0:T(8,128)(2,1)}, u32[]{:S(2)}) copy-start(bf16[1,2,1,2,384,384]{5,4,3,2,1,0:T(8,128)(2,1)} %param.7) | copy-start | bytes 3538948
  17.1 8.7 %copy-start.2 = (f32[1,384,384]{2,1,0:T(8,128)}, f32[1,384,384]{2,1,0:T(8,128)S(1)}, u32[]{:S(2)}) copy-start(f32[1,384,384]{2,1,0:T(8,128)S(1)} %get-tuple-element.7) | copy-start | bytes 1769476
  30.0 1.2 copy-start
  31.2 5.3 %collective-permute-start = (bf16[2,1,2,384,384]{4,3,0,2,1:T(8,128)(2,1)}, bf16[2,1,2,384,384]{4,3,0,2,1:T(8,128)(2,1)}, u32[]{:S(2)}, u32[]{:S(2)}) collective-permute-start(bf16[2,1,2,384,384]{4,3,0,2,1:T(8,128)(2,1)} %pad_maximum_fusion), channel_id=1, source_target_pairs={{0,4},{4,8},{8,12},{12,16},{16,20},{20,24},{24,28},{1,5},{5,9},{9,... | collective-permute-start | bytes 3538952 | tf_op jit(solution)/shard_map/ppermute | solution.py:17
  43.8 17.0 %copy-start.1 = (bf16[2,1,1,384,384]{4,3,0,2,1:T(8,128)(2,1)S(1)}, bf16[2,1,1,384,384]{4,3,0,2,1:T(8,128)(2,1)}, u32[]{:S(2)}) copy-start(bf16[2,1,1,384,384]{4,3,0,2,1:T(8,128)(2,1)} %copy-done) | copy-start | bytes 1769476
  44.0 19.0 %collective-permute-start.1 = (bf16[2,1,2,384,384]{4,3,0,2,1:T(8,128)(2,1)S(1)}, bf16[2,1,2,384,384]{4,3,0,2,1:T(8,128)(2,1)S(1)}, u32[]{:S(2)}, u32[]{:S(2)}) collective-permute-start(bf16[2,1,2,384,384]{4,3,0,2,1:T(8,128)(2,1)S(1)} %pad_maximum_fusion.1), channel_id=1, source_target_pairs={{0,4},{4,8},{8,12},{12,16},{16,20},{20,24},{24,28},{1,5},{5,9},{9,... | collective-permute-start | bytes 3538952 | tf_op jit(solution)/shard_map/ppermute | solution.py:17
  70.4 1.3 copy-start.6
  71.7 67.5 %collective-permute-start.2 = (bf16[1,2,384,384]{3,2,1,0:T(8,128)(2,1)S(1)}, bf16[1,2,384,384]{3,2,1,0:T(8,128)(2,1)S(1)}, u32[]{:S(2)}, u32[]{:S(2)}) collective-permute-start(bf16[1,2,384,384]{3,2,1,0:T(8,128)(2,1)S(1)} %bitcast.261), channel_id=1, source_target_pairs={{4,0},{8,4},{12,8},{16,12},{20,16},{24,20},{28,24},{5,1},{9,5},{13... | collective-permute-start | bytes 1769480 | tf_op jit(solution)/shard_map/ppermute | solution.py:17
  145.9 1.1 copy-start.3
Sparse Core Ops, SparseCore 0:
  71.8 61.2 all-reduce.2
where the time goes:
time: 157 us
  waiting for transfers between devices  61.7 us (39%)
  other arithmetic  27.7 us (18%)
  starting transfers between devices  21.8 us (14%)
  matrix products  20.2 us (13%)
  between operations  17.2 us (11%)
  local copies, waits for them, and re-layouts  8.43 us (5%)
    psum x1, waiting for transfers between devices, per_device(): lax.psum(illum_all.astype(jnp.bfloat16), 'freq').astype(jnp.float32)  59.8 us
    ppermute x3, starting transfers between devices, passed_along(): return lax.ppermute(block, axis, route)  21.8 us
    dot_general x4, matrix products, propagate(): jnp.dot(joined_rows, jnp.concatenate([shifted_real, shifted_imag], axis=1...  5.13 us
    dot_general x4, matrix products, propagate(): jnp.dot(jnp.concatenate([back_real, back_imag], axis=0), joined_cols, pre...  5.05 us
    dot_general x4, matrix products, propagate(): jnp.dot(jnp.concatenate([real_part, imag_part], axis=0), joined_cols, pre...  5.05 us
    dot_general x4, matrix products, propagate(): jnp.dot(joined_rows, jnp.concatenate([half_real, half_imag], axis=1), pre...  4.96 us
    another operation x6, other arithmetic, advance(): return jnp.stack([new_real, new_imag], axis=1)  4.86 us
    broadcast_in_dim x2, local copies, waits for them, and re-layouts, cell_slowness(): jnp.broadcast_to(block_slow[:, :, None, :, None], (count, blocks, BLOCK,...  4.38 us
  transfers between devices with their start and end apart: 4, of which 2 were waited for; matrix products, arithmetic and copies ran while one was open for 4% of the time, Pallas kernels for 0%

commit v1 on v0

--- a/solution.py
+++ b/solution.py
@@ -160,7 +160,7 @@
     illum_all = jnp.stack(illumination)
     image_total, illum_total = (
         lax.psum(image_all.astype(jnp.bfloat16), "freq").astype(jnp.float32),
-        lax.psum(illum_all.astype(jnp.bfloat16), "freq").astype(jnp.float32),
+        jnp.sum(lax.all_gather(illum_all.astype(jnp.bfloat16), "freq"), axis=0).astype(jnp.float32),
     )
     damping = jnp.mean(illum_total, axis=(1, 2))
     balanced = image_total / (illum_total + damping[:, None, None])

time: 157 us -> 183 us (1.17)
  waiting for transfers between devices: 61.7 us -> 87 us
    all_gather x0 -> x1, waiting for transfers between devices: none -> 40.6 us  [per_device(): lax.all_gather(illum_all.astype(jnp.bfloat16), 'freq')]
    psum x1, waiting for transfers between devices: 59.8 us -> 43.9 us  [per_device(): lax.psum(image_all.astype(jnp.bfloat16), 'freq').astype(jnp.float32)]
  transfers between devices with their start and end apart: 4 -> 5, of which waited for: 2 -> 3; matrix products, arithmetic and copies ran while one was open for 4% -> 4% of each run, Pallas kernels for 0% -> 0%
where the time goes in v1:
time: 183 us
  waiting for transfers between devices  87 us (48%)
  other arithmetic  28.2 us (15%)
  starting transfers between devices  21.9 us (12%)
  matrix products  20.2 us (11%)
  between operations  17.2 us (9%)
  local copies, waits for them, and re-layouts  8.44 us (5%)
    psum x1, waiting for transfers between devices, per_device(): lax.psum(image_all.astype(jnp.bfloat16), 'freq').astype(jnp.float32)  43.9 us
    all_gather x1, waiting for transfers between devices, per_device(): lax.all_gather(illum_all.astype(jnp.bfloat16), 'freq')  40.6 us
    ppermute x3, starting transfers between devices, passed_along(): return lax.ppermute(block, axis, route)  21.8 us
    dot_general x4, matrix products, propagate(): jnp.dot(joined_rows, jnp.concatenate([shifted_real, shifted_imag], axis=1...  5.12 us
    dot_general x4, matrix products, propagate(): jnp.dot(jnp.concatenate([back_real, back_imag], axis=0), joined_cols, pre...  5.05 us
    dot_general x4, matrix products, propagate(): jnp.dot(jnp.concatenate([real_part, imag_part], axis=0), joined_cols, pre...  5.04 us
    dot_general x4, matrix products, propagate(): jnp.dot(joined_rows, jnp.concatenate([half_real, half_imag], axis=1), pre...  4.96 us
    another operation x6, other arithmetic, advance(): return jnp.stack([new_real, new_imag], axis=1)  4.89 us
  transfers between devices with their start and end apart: 5, of which 3 were waited for; matrix products, arithmetic and copies ran while one was open for 4% of the time, Pallas kernels for 0%

profile of v1, /device:TPU:0, one launch (start us, length us, event | category | flops | bytes accessed | tf_op | source)
XLA Modules:
  0.0 182.9 jit_solution(16351738295677186470)
XLA Ops:
  7.2 2.6 %sine_convert_fusion = (bf16[384,384]{0,1:T(8,128)(2,1)S(1)}, bf16[384,384]{0,1:T(8,128)(2,1)S(1)}) fusion(), kind=kLoop, calls=%fused_computation.238 | loop fusion | flops 1622016 | bytes 589824 | tf_op jit(solution)/shard_map/convert_element_type | solution.py:25
  11.2 1.9 %broadcast_in_dim.6 = f32[12,32,12,32]{3,2,1,0:T(8,128)} broadcast(f32[12,12]{1,0:T(8,128)S(1)} %select_reduce_fusion), dimensions={0,2} | broadcast | bytes 590400 | tf_op jit(solution)/shard_map/broadcast_in_dim | solution.py:37
  13.1 2.5 %broadcast_in_dim.7 = f32[1,384,384]{2,1,0:T(8,128)S(1)} reshape(f32[12,32,12,32]{3,2,1,0:T(8,128)} %broadcast_in_dim.6) | data formatting | bytes 1179648 | tf_op jit(solution)/shard_map/broadcast_in_dim | solution.py:37
  18.1 1.4 convolution_bitcast_fusion.11
  19.8 2.6 %cosine_multiply_fusion.1 = (f32[384,384]{0,1:T(8,128)S(1)}, f32[384,384]{0,1:T(8,128)S(1)}) fusion(f32[384]{0:T(512)S(1)} %fusion.123, f32[]{:T(128)} %bitcast.11), kind=kLoop, calls=%fused_computation.234 | loop fusion | flops 1327104 | bytes 1181188 | tf_op jit(solution)/shard_map/vmap(vmap())/mul | solution.py:71
  22.3 1.4 convolution_bitcast_fusion.10
  24.1 1.4 convolution_bitcast_fusion.9
  25.8 2.3 %fusion.114 = (f32[384,384]{1,0:T(8,128)S(1)}, f32[384,384]{1,0:T(8,128)S(1)}) fusion(f32[1,384,384]{2,1,0:T(8,128)S(1)} %get-tuple-element.5, f32[]{:T(128)} %div.22, f32[]{:T(128)} %bitcast.264), kind=kLoop, calls=%fused_computation.246 | loop fusion | flops 294912 | bytes 1769480 | tf_op jit(solution)/shard_map/vmap(vmap())/mul | solution.py:95
  28.2 1.4 convolution_bitcast_fusion.8
  30.0 1.2 pad_maximum_fusion
  31.2 3.4 %collective-permute-start = (bf16[2,1,2,384,384]{4,3,0,2,1:T(8,128)(2,1)}, bf16[2,1,2,384,384]{4,3,0,2,1:T(8,128)(2,1)}, u32[]{:S(2)}, u32[]{:S(2)}) collective-permute-start(bf16[2,1,2,384,384]{4,3,0,2,1:T(8,128)(2,1)} %pad_maximum_fusion), channel_id=1, source_target_pairs={{0,4},{4,8},{8,12},{12,16},{16,20},{20,24},{24,28},{1,5},{5,9},{9,... | collective-permute-start | bytes 3538952 | tf_op jit(solution)/shard_map/ppermute | solution.py:17
  34.6 1.9 %fusion.141 = (bf16[1,2,1,2,384,384]{5,4,3,2,1,0:T(8,128)(2,1)S(1)}, bf16[1,2,1,2,384,384]{5,4,3,2,1,0:T(8,128)(2,1)S(1)}) fusion(bf16[2,2,1,2,384,384]{5,4,3,2,1,0:T(8,128)(2,1)} %param.8), kind=kLoop, calls=%fused_computation.281 | loop fusion | bytes 4718592 | tf_op jit(solution)/shard_map/slice | solution.py:158
  36.8 1.4 convolution_bitcast_fusion.7
  38.5 1.4 convolution_bitcast_fusion.6
  40.3 1.4 convolution_bitcast_fusion.5
  42.0 1.4 convolution_bitcast_fusion.4
  44.0 16.8 %collective-permute-start.1 = (bf16[2,1,2,384,384]{4,3,0,2,1:T(8,128)(2,1)S(1)}, bf16[2,1,2,384,384]{4,3,0,2,1:T(8,128)(2,1)S(1)}, u32[]{:S(2)}, u32[]{:S(2)}) collective-permute-start(bf16[2,1,2,384,384]{4,3,0,2,1:T(8,128)(2,1)S(1)} %pad_maximum_fusion.1), channel_id=1, source_target_pairs={{0,4},{4,8},{8,12},{12,16},{16,20},{20,24},{24,28},{1,5},{5,9},{9,... | collective-permute-start | bytes 3538952 | tf_op jit(solution)/shard_map/ppermute | solution.py:17
  61.2 1.8 collective-permute-done.1
  63.3 1.4 convolution_bitcast_fusion.3
  64.9 1.4 convolution_bitcast_fusion.2
  66.7 1.4 convolution_bitcast_fusion.1
  68.4 1.4 convolution_bitcast_fusion
  70.4 1.3 fusion.120
  72.5 1.6 collective-permute-start.2
  74.1 40.6 %all-gather.2.cloned.1.call-done = bf16[4,1,384,384]{3,2,1,0:T(8,128)(2,1)} async-done(((bf16[1,1,384,384]{3,2,1,0:T(8,128)(2,1)}), bf16[4,1,384,384]{3,2,1,0:T(8,128)(2,1)}) %all-gather.2.cloned.1.call-update) | async-done | bytes 1179664 | tf_op jit(solution)/shard_map/all_gather | solution.py:163
  114.7 1.5 reduce_sum.51
  117.7 43.9 %all-reduce.2.cloned.1.call-done = bf16[1,384,384]{2,1,0:T(8,128)(2,1)} async-done(((bf16[1,384,384]{2,1,0:T(8,128)(2,1)}), bf16[1,384,384]{2,1,0:T(8,128)(2,1)}) %all-reduce.2.cloned.1.call-update) | async-done | bytes 294928 | tf_op jit(solution)/shard_map/psum | solution.py:162
  161.6 1.7 multiply_reduce_fusion
  164.0 1.1 bitcast_convert_fusion
  167.1 3.1 %subtract_convert_fusion.7 = (bf16[1,384,384]{1,2,0:T(8,128)(2,1)S(1)}, bf16[1,384,384]{1,2,0:T(8,128)(2,1)S(1)}) fusion(f32[384]{0:T(512)S(1)} %fusion.123, f32[]{:T(128)} %bitcast.11, f32[768,1,768]{0,2,1:T(8,128)S(1)} %convolution_bitcast_fusion.12), kind=kLoop, calls=%fused_computation.223 | loop fusion | flops 2801664 | bytes 2953220 | tf_op jit(solution)/shard_map/vmap()/convert_element_type | solution.py:73
  172.8 2.3 %fusion.118 = (bf16[1,1,384,384]{3,2,1,0:T(8,128)(2,1)S(1)}, bf16[1,1,384,384]{3,2,1,0:T(8,128)(2,1)S(1)}) fusion(f32[1,384,384]{2,1,0:T(8,128)S(1)} %copy-done.3, f32[]{:T(128)} %div.22, f32[]{:T(128)} %bitcast.265, f32[1,768,768]{2,1,0:T(8,128)S(1)} %convolution_bitcast_fusion.13), kind=kLoop, calls=%fused_computation.253 | loop fusion | flops 1769472 | bytes 3538952 | tf_op jit(solution)/shard_map/stack | solution.py:116
  175.2 0.9 maximum_bitcast_fusion.32
  (56 shorter events, 13.7 us)
Async XLA Ops:
  7.2 107.5 %all-gather.2.cloned.1.call-start = ((), (), s32[]{:S(2)}) async-start(), calls=%async_computation.1 | async-start | bytes 1474560 | tf_op jit(solution)/shard_map/all_gather | solution.py:163
  13.1 3.3 %copy-start.5 = (f32[1,384,384]{2,1,0:T(8,128)S(1)}, f32[1,384,384]{2,1,0:T(8,128)}, u32[]{:S(2)}) copy-start(f32[1,384,384]{2,1,0:T(8,128)} %param.13) | copy-start | bytes 1769476
  15.6 2.2 %copy-start.4 = (bf16[1,2,1,2,384,384]{5,4,3,2,1,0:T(8,128)(2,1)S(1)}, bf16[1,2,1,2,384,384]{5,4,3,2,1,0:T(8,128)(2,1)}, u32[]{:S(2)}) copy-start(bf16[1,2,1,2,384,384]{5,4,3,2,1,0:T(8,128)(2,1)} %param.7) | copy-start | bytes 3538948
  17.1 8.7 %copy-start.2 = (f32[1,384,384]{2,1,0:T(8,128)}, f32[1,384,384]{2,1,0:T(8,128)S(1)}, u32[]{:S(2)}) copy-start(f32[1,384,384]{2,1,0:T(8,128)S(1)} %get-tuple-element.5) | copy-start | bytes 1769476
  30.0 1.2 copy-start
  31.2 5.3 %collective-permute-start = (bf16[2,1,2,384,384]{4,3,0,2,1:T(8,128)(2,1)}, bf16[2,1,2,384,384]{4,3,0,2,1:T(8,128)(2,1)}, u32[]{:S(2)}, u32[]{:S(2)}) collective-permute-start(bf16[2,1,2,384,384]{4,3,0,2,1:T(8,128)(2,1)} %pad_maximum_fusion), channel_id=1, source_target_pairs={{0,4},{4,8},{8,12},{12,16},{16,20},{20,24},{24,28},{1,5},{5,9},{9,... | collective-permute-start | bytes 3538952 | tf_op jit(solution)/shard_map/ppermute | solution.py:17
  43.8 17.0 %copy-start.1 = (bf16[2,1,1,384,384]{4,3,0,2,1:T(8,128)(2,1)S(1)}, bf16[2,1,1,384,384]{4,3,0,2,1:T(8,128)(2,1)}, u32[]{:S(2)}) copy-start(bf16[2,1,1,384,384]{4,3,0,2,1:T(8,128)(2,1)} %copy-done) | copy-start | bytes 1769476
  44.0 19.0 %collective-permute-start.1 = (bf16[2,1,2,384,384]{4,3,0,2,1:T(8,128)(2,1)S(1)}, bf16[2,1,2,384,384]{4,3,0,2,1:T(8,128)(2,1)S(1)}, u32[]{:S(2)}, u32[]{:S(2)}) collective-permute-start(bf16[2,1,2,384,384]{4,3,0,2,1:T(8,128)(2,1)S(1)} %pad_maximum_fusion.1), channel_id=1, source_target_pairs={{0,4},{4,8},{8,12},{12,16},{16,20},{20,24},{24,28},{1,5},{5,9},{9,... | collective-permute-start | bytes 3538952 | tf_op jit(solution)/shard_map/ppermute | solution.py:17
  70.4 2.1 %copy-start.6 = (bf16[1,1,2,384,384]{4,3,2,1,0:T(8,128)(2,1)S(1)}, bf16[1,1,2,384,384]{4,3,2,1,0:T(8,128)(2,1)}, u32[]{:S(2)}) copy-start(bf16[1,1,2,384,384]{4,3,2,1,0:T(8,128)(2,1)} %param.9) | copy-start | bytes 1769476
  71.7 89.8 %all-reduce.2.cloned.1.call-start = ((), (), s32[]{:S(2)}) async-start(), calls=%async_computation | async-start | bytes 589824 | tf_op jit(solution)/shard_map/psum | solution.py:162
  72.5 92.6 %collective-permute-start.2 = (bf16[1,2,384,384]{3,2,1,0:T(8,128)(2,1)S(1)}, bf16[1,2,384,384]{3,2,1,0:T(8,128)(2,1)S(1)}, u32[]{:S(2)}, u32[]{:S(2)}) collective-permute-start(bf16[1,2,384,384]{3,2,1,0:T(8,128)(2,1)S(1)} %bitcast.268), channel_id=1, source_target_pairs={{4,0},{8,4},{12,8},{16,12},{20,16},{24,20},{28,24},{5,1},{9,5},{13... | collective-permute-start | bytes 1769480 | tf_op jit(solution)/shard_map/ppermute | solution.py:17
  171.8 1.1 copy-start.3
Sparse Core Ops, SparseCore 0:
  71.9 42.7 all-gather.1
  118.2 43.3 all-reduce.1
